TPU v7x, 32 devices: a whole 2x2x4 slice. The times are simulated.
32 devices in a mesh: blk: 4 (over z), grp: 8 (over y, x, core).
Axes of the slice: x: 2, y: 2, z: 4, core: 2. Of those that a mesh axis runs over, the one named last changes fastest.
Arguments:
- position: float32 [3, 16384], P(None, ('blk', 'grp')), may hold values from -6 to 6
- velocity: float32 [3, 16384], P(None, ('blk', 'grp')), may hold values from -6 to 6
- accel_old: float32 [3, 16384], P(None, ('blk', 'grp')), may hold values from -6 to 6
- jerk_old: float32 [3, 16384], P(None, ('blk', 'grp')), may hold values from -6 to 6
- mass: float32 [16384], P(('blk', 'grp')), may hold values from 1e-07 to 1e-05
- elapsed: float32 [16384], P(('blk', 'grp')), may hold values from 0.1 to 1
- active_index: int32 [512], P(('blk', 'grp')), may hold values from 0 to 16383, as said below
Outputs:
- predicted: float32 [6, 16384], P(None, ('blk', 'grp'))
- accel: float32 [3, 512], P(None, ('blk', 'grp'))
- jerk: float32 [3, 512], P(None, ('blk', 'grp'))
Inputs may be any that keep to these rules, and one draw needn't show every extreme that they name: `active_index`: entries 16 * k to 16 * k + 15 are distinct stars of the range 512 * k to 512 * k + 511, for every k.
All inputs are finite; a program needn't handle non-finite values.
Results may differ from a plain program's by a relative error of at most 0.0003.
Values sent between devices are 32-bit elements; how exact they have to be, the bound alone decides.
A program may use at most 64 MiB of HBM per device.

v0:
```python
import math
import jax
import jax.numpy as jnp
from jax import lax
from jax.sharding import PartitionSpec as P

SOFTENING = 0.0001


def from_behind(shard, axis, by):
    count = lax.axis_size(axis)
    return lax.ppermute(shard, axis, [(i, (i + by) % count) for i in range(count)])


def predict(position, velocity, accel_old, jerk_old, elapsed):
    step_row = elapsed[None, :]
    half = step_row * step_row * 0.5
    sixth = half * step_row * (1.0 / 3.0)
    new_position = position + step_row * velocity + half * accel_old + sixth * jerk_old
    new_velocity = velocity + step_row * accel_old + half * jerk_old
    return jnp.concatenate([new_position, new_velocity], 0)


def interact(targets, sources, masses):
    columns = targets.shape[1]
    block_size = math.gcd(columns, 128)
    blocks = columns // block_size
    stacked = targets.reshape(6, blocks, block_size).transpose(1, 0, 2)

    def one_block(target_block):
        separation = sources[0:3][:, None, :] - target_block[0:3][:, :, None]
        relative = sources[3:6][:, None, :] - target_block[3:6][:, :, None]
        distance = jnp.sum(separation * separation, 0) + SOFTENING
        inverse = 1.0 / jnp.sqrt(distance)
        weight = masses[None, :] * inverse * inverse * inverse
        radial = 3.0 * jnp.sum(separation * relative, 0) / distance
        accel_part = jnp.sum(weight[None] * separation, 2)
        jerk_part = jnp.sum(weight[None] * (relative - radial[None] * separation), 2)
        return jnp.concatenate([accel_part, jerk_part], 0)

    result = lax.map(one_block, stacked)
    return result.transpose(1, 0, 2).reshape(6, columns)


def local(position, velocity, accel_old, jerk_old, mass, elapsed, active_index):
    predicted = predict(position, velocity, accel_old, jerk_old, elapsed)
    stars_here = position.shape[1]
    device = lax.axis_index("blk") * lax.axis_size("grp") + lax.axis_index("grp")
    offsets = active_index - device * stars_here
    owned_rows = jnp.take(predicted, offsets, axis=1)
    group_rows = lax.all_gather(owned_rows, "grp", axis=1, tiled=True)

    def circulate(number, carry):
        visitor, partial_value = carry
        partial_value = partial_value + interact(visitor, predicted, mass)
        return from_behind((visitor, partial_value), "blk", 1)

    start = jnp.zeros(group_rows.shape, jnp.float32)
    visitor, partial_value = lax.fori_loop(0, lax.axis_size("blk"), circulate, (group_rows, start))
    owned = lax.psum_scatter(partial_value, "grp", scatter_dimension=1, tiled=True)
    return (predicted, owned[0:3], owned[3:6])


def solution(mesh):
    in_specs = (
        P(None, ("blk", "grp")),
        P(None, ("blk", "grp")),
        P(None, ("blk", "grp")),
        P(None, ("blk", "grp")),
        P(("blk", "grp")),
        P(("blk", "grp")),
        P(("blk", "grp")),
    )
    out_specs = (P(None, ("blk", "grp")), P(None, ("blk", "grp")), P(None, ("blk", "grp")))
    return jax.shard_map(local, mesh=mesh, in_specs=in_specs, out_specs=out_specs, check_vma=False)
```

profile of v0, /device:TPU:0, one launch (start us, length us, event | category | flops | bytes accessed | tf_op | source)
XLA Modules:
  0.0 89.8 jit_solution(8160792300937886255)
XLA Ops:
  7.2 0.0 reduce-scatter.4.cloned.1.call-start
  7.3 0.6 copy-done.7
  7.9 0.0 copy-start.3
  7.9 0.7 copy-done.2
  8.6 0.0 copy-done.3
  8.7 0.0 copy-start
  8.7 0.1 copy.46
  8.8 0.4 copy-done
  9.3 0.6 gather_fusion
  9.8 0.1 broadcast_select_fusion
  9.9 0.1 copy.47
  10.0 10.6 %all-gather = f32[8,16,6]{1,2,0:T(8,128)S(1)} all-gather(f32[1,16,6]{1,2,0:T(8,128)S(1)} %bitcast.9), channel_id=1, replica_groups=mesh['blk'=4,'grp'=8] {'grp'}, dimensions={0}, use_global_device_ids=true | all-gather | bytes 3456 | tf_op jit(solution)/shard_map/all_gather | solution.py:51
  20.6 0.1 reshape.66
  20.7 0.7 copy-done.1
  21.3 26.4 %while.11 = (s32[]{:T(128)}, f32[6,128]{1,0:T(8,128)S(1)}, f32[6,128]{1,0:T(8,128)S(1)}, f32[3,512]{1,0:T(4,128)S(1)}, f32[512]{0:T(512)S(1)}, /*index=5*/f32[3,512]{1,0:T(4,128)S(1)}, s32[]{:T(128)}) while((s32[]{:T(128)}, f32[6,128]{1,0:T(8,128)S(1)}, f32[6,128]{1,0:T(8,128)S(1)}, f32[3,512]{1,0:T(4,128)S(1)}, f32[512]{0:T(512)S(1)}, ...), condition=%wide.region_5.6_spmd, body=%wide.region_0.5_spmd.sunk | while | flops 3015426 | bytes 2179229 | solution.py:59
  21.3 1.6 %collective-permute-start = (f32[6,128]{1,0:T(8,128)S(1)}, f32[6,128]{1,0:T(8,128)S(1)}, u32[]{:S(2)}, u32[]{:S(2)}) collective-permute-start(f32[6,128]{1,0:T(8,128)S(1)} %copy.57), channel_id=1, source_target_pairs={{0,8},{8,16},{16,24},{24,0},{1,9},{9,17},{17,25},{25,1},{2,10},{10... | collective-permute-start | bytes 9224 | tf_op jit(solution)/shard_map/while/body/eval_jaxpr/ppermute | solution.py:12
  22.9 0.2 fusion.11
  23.1 0.1 multiply_divide_fusion.2
  23.2 0.4 fusion.12
  23.6 1.6 %collective-permute-start.1 = (f32[6,128]{1,0:T(8,128)S(1)}, f32[6,128]{1,0:T(8,128)S(1)}, u32[]{:S(2)}, u32[]{:S(2)}) collective-permute-start(f32[6,128]{1,0:T(8,128)S(1)} %maximum_add_fusion.2), channel_id=1, source_target_pairs={{0,8},{8,16},{16,24},{24,0},{1,9},{9,17},{17,25},{25,1},{2,10},{10... | collective-permute-start | bytes 9224 | tf_op jit(solution)/shard_map/while/body/eval_jaxpr/ppermute | solution.py:12
  25.3 1.5 %collective-permute-done = f32[6,128]{1,0:T(8,128)S(1)} collective-permute-done((f32[6,128]{1,0:T(8,128)S(1)}, f32[6,128]{1,0:T(8,128)S(1)}, u32[]{:S(2)}, u32[]{:S(2)}) %collective-permute-start) | collective-permute-done | bytes 3104 | tf_op jit(solution)/shard_map/while/body/eval_jaxpr/ppermute | solution.py:12
  26.7 2.4 %collective-permute-done.1 = f32[6,128]{1,0:T(8,128)S(1)} collective-permute-done((f32[6,128]{1,0:T(8,128)S(1)}, f32[6,128]{1,0:T(8,128)S(1)}, u32[]{:S(2)}, u32[]{:S(2)}) %collective-permute-start.1) | collective-permute-done | bytes 3104 | tf_op jit(solution)/shard_map/while/body/eval_jaxpr/ppermute | solution.py:12
  29.1 0.0 collective-permute-start
  29.1 0.2 fusion.11
  29.3 0.1 multiply_divide_fusion.2
  29.4 0.4 fusion.12
  29.8 1.4 %collective-permute-start.1 = (f32[6,128]{1,0:T(8,128)S(1)}, f32[6,128]{1,0:T(8,128)S(1)}, u32[]{:S(2)}, u32[]{:S(2)}) collective-permute-start(f32[6,128]{1,0:T(8,128)S(1)} %maximum_add_fusion.2), channel_id=1, source_target_pairs={{0,8},{8,16},{16,24},{24,0},{1,9},{9,17},{17,25},{25,1},{2,10},{10... | collective-permute-start | bytes 9224 | tf_op jit(solution)/shard_map/while/body/eval_jaxpr/ppermute | solution.py:12
  31.2 3.3 %collective-permute-done = f32[6,128]{1,0:T(8,128)S(1)} collective-permute-done((f32[6,128]{1,0:T(8,128)S(1)}, f32[6,128]{1,0:T(8,128)S(1)}, u32[]{:S(2)}, u32[]{:S(2)}) %collective-permute-start) | collective-permute-done | bytes 3104 | tf_op jit(solution)/shard_map/while/body/eval_jaxpr/ppermute | solution.py:12
  34.5 0.8 collective-permute-done.1
  35.3 0.0 collective-permute-start
  35.3 0.2 fusion.11
  35.5 0.1 multiply_divide_fusion.2
  35.6 0.4 fusion.12
  36.0 0.9 %collective-permute-start.1 = (f32[6,128]{1,0:T(8,128)S(1)}, f32[6,128]{1,0:T(8,128)S(1)}, u32[]{:S(2)}, u32[]{:S(2)}) collective-permute-start(f32[6,128]{1,0:T(8,128)S(1)} %maximum_add_fusion.2), channel_id=1, source_target_pairs={{0,8},{8,16},{16,24},{24,0},{1,9},{9,17},{17,25},{25,1},{2,10},{10... | collective-permute-start | bytes 9224 | tf_op jit(solution)/shard_map/while/body/eval_jaxpr/ppermute | solution.py:12
  37.0 3.8 %collective-permute-done = f32[6,128]{1,0:T(8,128)S(1)} collective-permute-done((f32[6,128]{1,0:T(8,128)S(1)}, f32[6,128]{1,0:T(8,128)S(1)}, u32[]{:S(2)}, u32[]{:S(2)}) %collective-permute-start) | collective-permute-done | bytes 3104 | tf_op jit(solution)/shard_map/while/body/eval_jaxpr/ppermute | solution.py:12
  40.7 0.8 collective-permute-done.1
  41.5 0.2 fusion.11
  41.7 0.1 multiply_divide_fusion.2
  41.8 0.4 fusion.12
  42.2 1.4 %collective-permute-start.1 = (f32[6,128]{1,0:T(8,128)S(1)}, f32[6,128]{1,0:T(8,128)S(1)}, u32[]{:S(2)}, u32[]{:S(2)}) collective-permute-start(f32[6,128]{1,0:T(8,128)S(1)} %maximum_add_fusion.2), channel_id=1, source_target_pairs={{0,8},{8,16},{16,24},{24,0},{1,9},{9,17},{17,25},{25,1},{2,10},{10... | collective-permute-start | bytes 9224 | tf_op jit(solution)/shard_map/while/body/eval_jaxpr/ppermute | solution.py:12
  43.6 3.3 %collective-permute-done = f32[6,128]{1,0:T(8,128)S(1)} collective-permute-done((f32[6,128]{1,0:T(8,128)S(1)}, f32[6,128]{1,0:T(8,128)S(1)}, u32[]{:S(2)}, u32[]{:S(2)}) %collective-permute-start) | collective-permute-done | bytes 3104 | tf_op jit(solution)/shard_map/while/body/eval_jaxpr/ppermute | solution.py:12
  46.9 0.8 collective-permute-done.1
  47.7 0.7 copy.49
  48.4 0.0 reduce-scatter.4.cloned.1.call-update
  48.5 32.4 %reduce-scatter.4.cloned.1.call-done = f32[16,6]{1,0:T(8,128)} async-done(((f32[128,6]{1,0:T(8,128)}), f32[16,6]{1,0:T(8,128)}) %reduce-scatter.4.cloned.1.call-update) | async-done | bytes 400
  80.8 0.8 fusion.6
  81.7 0.7 copy.52
  82.3 0.7 copy.51
  (29 shorter events, 0.1 us)
Async XLA Ops:
  7.2 73.7 %reduce-scatter.4.cloned.1.call-start = ((), (), s32[]{:S(2)}) async-start(), calls=%async_computation.1 | async-start | bytes 73728
  7.2 1.4 %copy-start.6 = (f32[3,512]{1,0:T(4,128)S(1)}, f32[3,512]{1,0:T(4,128)}, u32[]{:S(2)}) copy-start(f32[3,512]{1,0:T(4,128)} %param.10) | copy-start | bytes 18436
  7.2 1.4 %copy-start.5 = (f32[3,512]{1,0:T(4,128)S(1)}, f32[3,512]{1,0:T(4,128)}, u32[]{:S(2)}) copy-start(f32[3,512]{1,0:T(4,128)} %param.9) | copy-start | bytes 18436
  7.2 0.7 copy-start.7
  7.2 1.4 %copy-start.4 = (f32[3,512]{1,0:T(4,128)S(1)}, f32[3,512]{1,0:T(4,128)}, u32[]{:S(2)}) copy-start(f32[3,512]{1,0:T(4,128)} %param.11) | copy-start | bytes 18436
  7.9 0.7 copy-start.2
  7.9 0.7 copy-start.3
  8.7 0.6 copy-start
  20.7 0.7 copy-start.1
  21.3 5.4 %collective-permute-start = (f32[6,128]{1,0:T(8,128)S(1)}, f32[6,128]{1,0:T(8,128)S(1)}, u32[]{:S(2)}, u32[]{:S(2)}) collective-permute-start(f32[6,128]{1,0:T(8,128)S(1)} %copy.57), channel_id=1, source_target_pairs={{0,8},{8,16},{16,24},{24,0},{1,9},{9,17},{17,25},{25,1},{2,10},{10... | collective-permute-start | bytes 9224 | tf_op jit(solution)/shard_map/while/body/eval_jaxpr/ppermute | solution.py:12
  23.6 5.5 %collective-permute-start.1 = (f32[6,128]{1,0:T(8,128)S(1)}, f32[6,128]{1,0:T(8,128)S(1)}, u32[]{:S(2)}, u32[]{:S(2)}) collective-permute-start(f32[6,128]{1,0:T(8,128)S(1)} %maximum_add_fusion.2), channel_id=1, source_target_pairs={{0,8},{8,16},{16,24},{24,0},{1,9},{9,17},{17,25},{25,1},{2,10},{10... | collective-permute-start | bytes 9224 | tf_op jit(solution)/shard_map/while/body/eval_jaxpr/ppermute | solution.py:12
  29.1 5.4 %collective-permute-start = (f32[6,128]{1,0:T(8,128)S(1)}, f32[6,128]{1,0:T(8,128)S(1)}, u32[]{:S(2)}, u32[]{:S(2)}) collective-permute-start(f32[6,128]{1,0:T(8,128)S(1)} %copy.57), channel_id=1, source_target_pairs={{0,8},{8,16},{16,24},{24,0},{1,9},{9,17},{17,25},{25,1},{2,10},{10... | collective-permute-start | bytes 9224 | tf_op jit(solution)/shard_map/while/body/eval_jaxpr/ppermute | solution.py:12
  29.8 5.5 %collective-permute-start.1 = (f32[6,128]{1,0:T(8,128)S(1)}, f32[6,128]{1,0:T(8,128)S(1)}, u32[]{:S(2)}, u32[]{:S(2)}) collective-permute-start(f32[6,128]{1,0:T(8,128)S(1)} %maximum_add_fusion.2), channel_id=1, source_target_pairs={{0,8},{8,16},{16,24},{24,0},{1,9},{9,17},{17,25},{25,1},{2,10},{10... | collective-permute-start | bytes 9224 | tf_op jit(solution)/shard_map/while/body/eval_jaxpr/ppermute | solution.py:12
  35.3 5.4 %collective-permute-start = (f32[6,128]{1,0:T(8,128)S(1)}, f32[6,128]{1,0:T(8,128)S(1)}, u32[]{:S(2)}, u32[]{:S(2)}) collective-permute-start(f32[6,128]{1,0:T(8,128)S(1)} %copy.57), channel_id=1, source_target_pairs={{0,8},{8,16},{16,24},{24,0},{1,9},{9,17},{17,25},{25,1},{2,10},{10... | collective-permute-start | bytes 9224 | tf_op jit(solution)/shard_map/while/body/eval_jaxpr/ppermute | solution.py:12
  36.0 5.5 %collective-permute-start.1 = (f32[6,128]{1,0:T(8,128)S(1)}, f32[6,128]{1,0:T(8,128)S(1)}, u32[]{:S(2)}, u32[]{:S(2)}) collective-permute-start(f32[6,128]{1,0:T(8,128)S(1)} %maximum_add_fusion.2), channel_id=1, source_target_pairs={{0,8},{8,16},{16,24},{24,0},{1,9},{9,17},{17,25},{25,1},{2,10},{10... | collective-permute-start | bytes 9224 | tf_op jit(solution)/shard_map/while/body/eval_jaxpr/ppermute | solution.py:12
  41.5 5.4 %collective-permute-start = (f32[6,128]{1,0:T(8,128)S(1)}, f32[6,128]{1,0:T(8,128)S(1)}, u32[]{:S(2)}, u32[]{:S(2)}) collective-permute-start(f32[6,128]{1,0:T(8,128)S(1)} %copy.57), channel_id=1, source_target_pairs={{0,8},{8,16},{16,24},{24,0},{1,9},{9,17},{17,25},{25,1},{2,10},{10... | collective-permute-start | bytes 9224 | tf_op jit(solution)/shard_map/while/body/eval_jaxpr/ppermute | solution.py:12
  42.2 5.5 %collective-permute-start.1 = (f32[6,128]{1,0:T(8,128)S(1)}, f32[6,128]{1,0:T(8,128)S(1)}, u32[]{:S(2)}, u32[]{:S(2)}) collective-permute-start(f32[6,128]{1,0:T(8,128)S(1)} %maximum_add_fusion.2), channel_id=1, source_target_pairs={{0,8},{8,16},{16,24},{24,0},{1,9},{9,17},{17,25},{25,1},{2,10},{10... | collective-permute-start | bytes 9224 | tf_op jit(solution)/shard_map/while/body/eval_jaxpr/ppermute | solution.py:12
Sparse Core Ops, SparseCore 0:
  48.6 32.2 reduce-scatter.3
where the time goes:
time: 90.2 us; the launch traced here: 89.8 us
  waiting for transfers between devices  48.9 us (54%)
  between operations  14.1 us (16%)
  blocking collectives  10.6 us (12%)
  starting transfers between devices  6.96 us (8%)
  local copies, waits for them, and re-layouts  6.22 us (7%)
  other arithmetic  2.95 us (3%)
    unnamed x2, waiting for transfers between devices  32.4 us
    ppermute x8, waiting for transfers between devices, from_behind(): lax.ppermute(shard, axis, [(i, (i + by) % count) for i in range(count)])  16.5 us
    all_gather x1, blocking collectives, local(): group_rows = lax.all_gather(owned_rows, 'grp', axis=1, tiled=True)  10.6 us
    ppermute x8, starting transfers between devices, from_behind(): lax.ppermute(shard, axis, [(i, (i + by) % count) for i in range(count)])  6.93 us
    unnamed x20, local copies, waits for them, and re-layouts  4.56 us
  transfers between devices with their start and end apart: 9, of which 9 were waited for; matrix products, arithmetic and copies ran while one was open for 3% of the time, Pallas kernels for 0%

commit v1 on v0

--- a/solution.py
+++ b/solution.py
@@ -5,6 +5,12 @@
 from jax.sharding import PartitionSpec as P
 
 SOFTENING = 0.0001
+
+
+def in_order(blocks, dim):
+    blocks = jnp.moveaxis(blocks, 0, dim)
+    dims = blocks.shape
+    return blocks.reshape(*dims[:dim], dims[dim] * dims[dim + 1], *dims[dim + 2 :])
 
 
 def from_behind(shard, axis, by):
@@ -48,7 +54,19 @@
     device = lax.axis_index("blk") * lax.axis_size("grp") + lax.axis_index("grp")
     offsets = active_index - device * stars_here
     owned_rows = jnp.take(predicted, offsets, axis=1)
-    group_rows = lax.all_gather(owned_rows, "grp", axis=1, tiled=True)
+    count_2 = lax.axis_size("grp")
+    pairs = [(i_2, (i_2 + 1) % count_2) for i_2 in range(count_2)]
+    back = [(b, a) for a, b in pairs]
+    lower, upper = ([], [])
+    for step in range(count_2 - 1):
+        if step % 2 == 0:
+            lower.append(lax.ppermute(lower[-1] if lower else owned_rows, "grp", pairs))
+        else:
+            upper.append(lax.ppermute(upper[-1] if upper else owned_rows, "grp", back))
+    blocks_2 = jnp.stack([*lower[::-1], owned_rows, *upper])
+    shift = lax.axis_index("grp") - len(lower)
+    blocks_2 = blocks_2[(jnp.arange(count_2) - shift) % count_2]
+    group_rows = in_order(blocks_2, 1)
 
     def circulate(number, carry):
         visitor, partial_value = carry

time: 90.2 us -> 98.4 us (1.091)
  blocking collectives: 10.6 us -> 0 us
  starting transfers between devices: 6.96 us -> 16.4 us
  waiting for transfers between devices: 48.9 us -> 56.4 us
  local copies, waits for them, and re-layouts: 6.22 us -> 7.35 us
    all_gather x1 -> x0, blocking collectives: 10.6 us -> none  [local(): group_rows = lax.all_gather(owned_rows, 'grp', axis=1, tiled=True)]
    ppermute x0 -> x7, starting transfers between devices: none -> 8.68 us  [the longest x3 8.18 us: local(): upper.append(lax.ppermute(upper[-1] if upper else owned_rows, 'grp', back))]
    ppermute x0 -> x7, waiting for transfers between devices: none -> 7.36 us  [the longest x4 7.26 us: local(): lower.append(lax.ppermute(lower[-1] if lower else owned_rows, 'grp', pairs))]
    unnamed x20 -> x23, local copies, waits for them, and re-layouts: 4.56 us -> 4.51 us
  transfers between devices with their start and end apart: 9 -> 16, of which waited for: 9 -> 14; matrix products, arithmetic and copies ran while one was open for 3% -> 3% of each run, Pallas kernels for 0% -> 0%
where the time goes in v1:
time: 98.4 us; the launch traced here: 98 us
  waiting for transfers between devices  56.4 us (57%)
  starting transfers between devices  16.4 us (17%)
  between operations  14.2 us (14%)
  local copies, waits for them, and re-layouts  7.35 us (7%)
  other arithmetic  3.67 us (4%)
    unnamed x2, waiting for transfers between devices  32.5 us
    ppermute x8, waiting for transfers between devices, from_behind(): lax.ppermute(shard, axis, [(i, (i + by) % count) for i in range(count)])  16.5 us
    ppermute x3, starting transfers between devices, local(): upper.append(lax.ppermute(upper[-1] if upper else owned_rows, 'grp', back))  8.18 us
    ppermute x8, starting transfers between devices, from_behind(): lax.ppermute(shard, axis, [(i, (i + by) % count) for i in range(count)])  7.68 us
    ppermute x4, waiting for transfers between devices, local(): lower.append(lax.ppermute(lower[-1] if lower else owned_rows, 'grp', pairs))  7.26 us
    unnamed x23, local copies, waits for them, and re-layouts  4.51 us
  transfers between devices with their start and end apart: 16, of which 14 were waited for; matrix products, arithmetic and copies ran while one was open for 3% of the time, Pallas kernels for 0%

profile of v1, /device:TPU:0, one launch (start us, length us, event | category | flops | bytes accessed | tf_op | source)
XLA Modules:
  0.0 98.0 jit_solution(16678820844369142173)
XLA Ops:
  7.2 0.6 copy-done.6
  7.9 0.7 copy-done.2
  8.6 0.7 multiply_add_fusion.1
  9.3 0.1 copy.67
  9.5 0.4 copy-done
  9.9 0.6 gather_fusion
  10.6 0.5 collective-permute-start.2
  11.1 2.9 %collective-permute-start.6 = (f32[6,16]{0,1:T(8,128)S(1)}, f32[6,16]{0,1:T(8,128)S(1)}, u32[]{:S(2)}, u32[]{:S(2)}) collective-permute-start(f32[6,16]{0,1:T(8,128)S(1)} %broadcast_select_fusion), channel_id=1, source_target_pairs={{1,0},{2,1},{3,2},{4,3},{5,4},{6,5},{7,6},{0,7},{9,8},{10,9},{11,1... | collective-permute-start | bytes 1160 | tf_op jit(solution)/shard_map/ppermute | solution.py:65
  14.0 1.3 %collective-permute-done.2 = f32[6,16]{0,1:T(8,128)S(1)} collective-permute-done((f32[6,16]{0,1:T(8,128)S(1)}, f32[6,16]{0,1:T(8,128)S(1)}, u32[]{:S(2)}, u32[]{:S(2)}) %collective-permute-start.2) | collective-permute-done | bytes 416 | tf_op jit(solution)/shard_map/ppermute | solution.py:63
  15.4 2.6 %collective-permute-start.7 = (f32[6,16]{0,1:T(8,128)S(1)}, f32[6,16]{0,1:T(8,128)S(1)}, u32[]{:S(2)}, u32[]{:S(2)}) collective-permute-start(f32[6,16]{0,1:T(8,128)S(1)} %collective-permute-done.6), channel_id=1, source_target_pairs={{1,0},{2,1},{3,2},{4,3},{5,4},{6,5},{7,6},{0,7},{9,8},{10,9},{11,1... | collective-permute-start | bytes 1160 | tf_op jit(solution)/shard_map/ppermute | solution.py:65
  18.0 1.3 %collective-permute-done.3 = f32[6,16]{0,1:T(8,128)S(1)} collective-permute-done((f32[6,16]{0,1:T(8,128)S(1)}, f32[6,16]{0,1:T(8,128)S(1)}, u32[]{:S(2)}, u32[]{:S(2)}) %collective-permute-start.3) | collective-permute-done | bytes 416 | tf_op jit(solution)/shard_map/ppermute | solution.py:63
  19.3 0.1 copy.72
  19.4 2.6 %collective-permute-start.8 = (f32[6,16]{0,1:T(8,128)S(1)}, f32[6,16]{0,1:T(8,128)S(1)}, u32[]{:S(2)}, u32[]{:S(2)}) collective-permute-start(f32[6,16]{0,1:T(8,128)S(1)} %collective-permute-done.7), channel_id=1, source_target_pairs={{1,0},{2,1},{3,2},{4,3},{5,4},{6,5},{7,6},{0,7},{9,8},{10,9},{11,1... | collective-permute-start | bytes 1160 | tf_op jit(solution)/shard_map/ppermute | solution.py:65
  22.0 1.2 %collective-permute-done.4 = f32[6,16]{0,1:T(8,128)S(1)} collective-permute-done((f32[6,16]{0,1:T(8,128)S(1)}, f32[6,16]{0,1:T(8,128)S(1)}, u32[]{:S(2)}, u32[]{:S(2)}) %collective-permute-start.4) | collective-permute-done | bytes 416 | tf_op jit(solution)/shard_map/ppermute | solution.py:63
  23.7 3.5 %collective-permute-done.5 = f32[6,16]{0,1:T(8,128)S(1)} collective-permute-done((f32[6,16]{0,1:T(8,128)S(1)}, f32[6,16]{0,1:T(8,128)S(1)}, u32[]{:S(2)}, u32[]{:S(2)}) %collective-permute-start.5) | collective-permute-done | bytes 416 | tf_op jit(solution)/shard_map/ppermute | solution.py:63
  27.3 0.6 gather_fusion.1
  28.0 0.7 copy-done.1
  28.7 27.1 %while.11 = (s32[]{:T(128)}, f32[6,128]{1,0:T(8,128)S(1)}, f32[6,128]{1,0:T(8,128)S(1)}, f32[3,512]{1,0:T(4,128)S(1)}, f32[512]{0:T(512)S(1)}, /*index=5*/f32[3,512]{1,0:T(4,128)S(1)}, s32[]{:T(128)}) while((s32[]{:T(128)}, f32[6,128]{1,0:T(8,128)S(1)}, f32[6,128]{1,0:T(8,128)S(1)}, f32[3,512]{1,0:T(4,128)S(1)}, f32[512]{0:T(512)S(1)}, ...), condition=%wide.region_5.6_spmd, body=%wide.region_0.5_spmd.sunk | while | flops 3015426 | bytes 2179229 | solution.py:77
  28.7 2.3 %collective-permute-start = (f32[6,128]{1,0:T(8,128)S(1)}, f32[6,128]{1,0:T(8,128)S(1)}, u32[]{:S(2)}, u32[]{:S(2)}) collective-permute-start(f32[6,128]{1,0:T(8,128)S(1)} %copy.92), channel_id=1, source_target_pairs={{0,8},{8,16},{16,24},{24,0},{1,9},{9,17},{17,25},{25,1},{2,10},{10... | collective-permute-start | bytes 9224 | tf_op jit(solution)/shard_map/while/body/eval_jaxpr/ppermute | solution.py:18
  31.0 0.2 fusion.13
  31.2 0.1 multiply_divide_fusion.2
  31.3 0.4 fusion.14
  31.7 1.6 %collective-permute-start.1 = (f32[6,128]{1,0:T(8,128)S(1)}, f32[6,128]{1,0:T(8,128)S(1)}, u32[]{:S(2)}, u32[]{:S(2)}) collective-permute-start(f32[6,128]{1,0:T(8,128)S(1)} %maximum_add_fusion.2), channel_id=1, source_target_pairs={{0,8},{8,16},{16,24},{24,0},{1,9},{9,17},{17,25},{25,1},{2,10},{10... | collective-permute-start | bytes 9224 | tf_op jit(solution)/shard_map/while/body/eval_jaxpr/ppermute | solution.py:18
  33.4 1.2 %collective-permute-done = f32[6,128]{1,0:T(8,128)S(1)} collective-permute-done((f32[6,128]{1,0:T(8,128)S(1)}, f32[6,128]{1,0:T(8,128)S(1)}, u32[]{:S(2)}, u32[]{:S(2)}) %collective-permute-start) | collective-permute-done | bytes 3104 | tf_op jit(solution)/shard_map/while/body/eval_jaxpr/ppermute | solution.py:18
  34.6 2.6 %collective-permute-done.1 = f32[6,128]{1,0:T(8,128)S(1)} collective-permute-done((f32[6,128]{1,0:T(8,128)S(1)}, f32[6,128]{1,0:T(8,128)S(1)}, u32[]{:S(2)}, u32[]{:S(2)}) %collective-permute-start.1) | collective-permute-done | bytes 3104 | tf_op jit(solution)/shard_map/while/body/eval_jaxpr/ppermute | solution.py:18
  37.2 0.2 fusion.13
  37.4 0.1 multiply_divide_fusion.2
  37.5 0.4 fusion.14
  37.9 1.4 %collective-permute-start.1 = (f32[6,128]{1,0:T(8,128)S(1)}, f32[6,128]{1,0:T(8,128)S(1)}, u32[]{:S(2)}, u32[]{:S(2)}) collective-permute-start(f32[6,128]{1,0:T(8,128)S(1)} %maximum_add_fusion.2), channel_id=1, source_target_pairs={{0,8},{8,16},{16,24},{24,0},{1,9},{9,17},{17,25},{25,1},{2,10},{10... | collective-permute-start | bytes 9224 | tf_op jit(solution)/shard_map/while/body/eval_jaxpr/ppermute | solution.py:18
  39.3 3.3 %collective-permute-done = f32[6,128]{1,0:T(8,128)S(1)} collective-permute-done((f32[6,128]{1,0:T(8,128)S(1)}, f32[6,128]{1,0:T(8,128)S(1)}, u32[]{:S(2)}, u32[]{:S(2)}) %collective-permute-start) | collective-permute-done | bytes 3104 | tf_op jit(solution)/shard_map/while/body/eval_jaxpr/ppermute | solution.py:18
  42.6 0.8 collective-permute-done.1
  43.4 0.2 fusion.13
  43.6 0.1 multiply_divide_fusion.2
  43.7 0.4 fusion.14
  44.1 0.9 collective-permute-start.1
  45.0 3.8 %collective-permute-done = f32[6,128]{1,0:T(8,128)S(1)} collective-permute-done((f32[6,128]{1,0:T(8,128)S(1)}, f32[6,128]{1,0:T(8,128)S(1)}, u32[]{:S(2)}, u32[]{:S(2)}) %collective-permute-start) | collective-permute-done | bytes 3104 | tf_op jit(solution)/shard_map/while/body/eval_jaxpr/ppermute | solution.py:18
  48.8 0.8 collective-permute-done.1
  49.6 0.2 fusion.13
  49.8 0.1 multiply_divide_fusion.2
  49.9 0.4 fusion.14
  50.3 1.4 %collective-permute-start.1 = (f32[6,128]{1,0:T(8,128)S(1)}, f32[6,128]{1,0:T(8,128)S(1)}, u32[]{:S(2)}, u32[]{:S(2)}) collective-permute-start(f32[6,128]{1,0:T(8,128)S(1)} %maximum_add_fusion.2), channel_id=1, source_target_pairs={{0,8},{8,16},{16,24},{24,0},{1,9},{9,17},{17,25},{25,1},{2,10},{10... | collective-permute-start | bytes 9224 | tf_op jit(solution)/shard_map/while/body/eval_jaxpr/ppermute | solution.py:18
  51.7 3.3 %collective-permute-done = f32[6,128]{1,0:T(8,128)S(1)} collective-permute-done((f32[6,128]{1,0:T(8,128)S(1)}, f32[6,128]{1,0:T(8,128)S(1)}, u32[]{:S(2)}, u32[]{:S(2)}) %collective-permute-start) | collective-permute-done | bytes 3104 | tf_op jit(solution)/shard_map/while/body/eval_jaxpr/ppermute | solution.py:18
  55.0 0.8 collective-permute-done.1
  55.8 0.7 copy.77
  56.5 32.5 %reduce-scatter.4.cloned.1.call-done = f32[16,6]{1,0:T(8,128)} async-done(((f32[128,6]{1,0:T(8,128)}), f32[16,6]{1,0:T(8,128)}) %reduce-scatter.4.cloned.1.call-update) | async-done | bytes 400
  89.0 0.8 fusion.8
  89.9 0.7 copy.80
  90.5 0.7 copy.79
  (58 shorter events, 1.1 us)
Async XLA Ops:
  7.2 81.9 %reduce-scatter.4.cloned.1.call-start = ((), (), s32[]{:S(2)}) async-start(), calls=%async_computation.1 | async-start | bytes 73728
  7.2 1.4 %copy-start.5 = (f32[3,512]{1,0:T(4,128)S(1)}, f32[3,512]{1,0:T(4,128)}, u32[]{:S(2)}) copy-start(f32[3,512]{1,0:T(4,128)} %param.9) | copy-start | bytes 18436
  7.2 0.7 copy-start.6
  7.2 1.4 %copy-start.4 = (f32[3,512]{1,0:T(4,128)S(1)}, f32[3,512]{1,0:T(4,128)}, u32[]{:S(2)}) copy-start(f32[3,512]{1,0:T(4,128)} %param.11) | copy-start | bytes 18436
  7.9 0.7 copy-start.2
  7.9 0.7 copy-start.3
  9.3 0.6 copy-start
  10.6 4.7 %collective-permute-start.2 = (f32[6,16]{0,1:T(8,128)S(1)}, f32[6,16]{0,1:T(8,128)S(1)}, u32[]{:S(2)}, u32[]{:S(2)}) collective-permute-start(f32[6,16]{0,1:T(8,128)S(1)} %broadcast_select_fusion), channel_id=1, source_target_pairs={{0,1},{1,2},{2,3},{3,4},{4,5},{5,6},{6,7},{7,0},{8,9},{9,10},{10,1... | collective-permute-start | bytes 1160 | tf_op jit(solution)/shard_map/ppermute | solution.py:63
  11.1 4.3 %collective-permute-start.6 = (f32[6,16]{0,1:T(8,128)S(1)}, f32[6,16]{0,1:T(8,128)S(1)}, u32[]{:S(2)}, u32[]{:S(2)}) collective-permute-start(f32[6,16]{0,1:T(8,128)S(1)} %broadcast_select_fusion), channel_id=1, source_target_pairs={{1,0},{2,1},{3,2},{4,3},{5,4},{6,5},{7,6},{0,7},{9,8},{10,9},{11,1... | collective-permute-start | bytes 1160 | tf_op jit(solution)/shard_map/ppermute | solution.py:65
  15.3 4.0 %collective-permute-start.3 = (f32[6,16]{0,1:T(8,128)S(1)}, f32[6,16]{0,1:T(8,128)S(1)}, u32[]{:S(2)}, u32[]{:S(2)}) collective-permute-start(f32[6,16]{0,1:T(8,128)S(1)} %collective-permute-done.2), channel_id=1, source_target_pairs={{0,1},{1,2},{2,3},{3,4},{4,5},{5,6},{6,7},{7,0},{8,9},{9,10},{10,1... | collective-permute-start | bytes 1160 | tf_op jit(solution)/shard_map/ppermute | solution.py:63
  15.4 4.0 %collective-permute-start.7 = (f32[6,16]{0,1:T(8,128)S(1)}, f32[6,16]{0,1:T(8,128)S(1)}, u32[]{:S(2)}, u32[]{:S(2)}) collective-permute-start(f32[6,16]{0,1:T(8,128)S(1)} %collective-permute-done.6), channel_id=1, source_target_pairs={{1,0},{2,1},{3,2},{4,3},{5,4},{6,5},{7,6},{0,7},{9,8},{10,9},{11,1... | collective-permute-start | bytes 1160 | tf_op jit(solution)/shard_map/ppermute | solution.py:65
  19.3 4.0 %collective-permute-start.4 = (f32[6,16]{0,1:T(8,128)S(1)}, f32[6,16]{0,1:T(8,128)S(1)}, u32[]{:S(2)}, u32[]{:S(2)}) collective-permute-start(f32[6,16]{0,1:T(8,128)S(1)} %collective-permute-done.3), channel_id=1, source_target_pairs={{0,1},{1,2},{2,3},{3,4},{4,5},{5,6},{6,7},{7,0},{8,9},{9,10},{10,1... | collective-permute-start | bytes 1160 | tf_op jit(solution)/shard_map/ppermute | solution.py:63
  19.4 4.3 %collective-permute-start.8 = (f32[6,16]{0,1:T(8,128)S(1)}, f32[6,16]{0,1:T(8,128)S(1)}, u32[]{:S(2)}, u32[]{:S(2)}) collective-permute-start(f32[6,16]{0,1:T(8,128)S(1)} %collective-permute-done.7), channel_id=1, source_target_pairs={{1,0},{2,1},{3,2},{4,3},{5,4},{6,5},{7,6},{0,7},{9,8},{10,9},{11,1... | collective-permute-start | bytes 1160 | tf_op jit(solution)/shard_map/ppermute | solution.py:65
  23.2 4.0 %collective-permute-start.5 = (f32[6,16]{0,1:T(8,128)S(1)}, f32[6,16]{0,1:T(8,128)S(1)}, u32[]{:S(2)}, u32[]{:S(2)}) collective-permute-start(f32[6,16]{0,1:T(8,128)S(1)} %collective-permute-done.4), channel_id=1, source_target_pairs={{0,1},{1,2},{2,3},{3,4},{4,5},{5,6},{6,7},{7,0},{8,9},{9,10},{10,1... | collective-permute-start | bytes 1160 | tf_op jit(solution)/shard_map/ppermute | solution.py:63
  28.0 0.7 copy-start.1
  28.7 5.9 %collective-permute-start = (f32[6,128]{1,0:T(8,128)S(1)}, f32[6,128]{1,0:T(8,128)S(1)}, u32[]{:S(2)}, u32[]{:S(2)}) collective-permute-start(f32[6,128]{1,0:T(8,128)S(1)} %copy.92), channel_id=1, source_target_pairs={{0,8},{8,16},{16,24},{24,0},{1,9},{9,17},{17,25},{25,1},{2,10},{10... | collective-permute-start | bytes 9224 | tf_op jit(solution)/shard_map/while/body/eval_jaxpr/ppermute | solution.py:18
  31.7 5.5 %collective-permute-start.1 = (f32[6,128]{1,0:T(8,128)S(1)}, f32[6,128]{1,0:T(8,128)S(1)}, u32[]{:S(2)}, u32[]{:S(2)}) collective-permute-start(f32[6,128]{1,0:T(8,128)S(1)} %maximum_add_fusion.2), channel_id=1, source_target_pairs={{0,8},{8,16},{16,24},{24,0},{1,9},{9,17},{17,25},{25,1},{2,10},{10... | collective-permute-start | bytes 9224 | tf_op jit(solution)/shard_map/while/body/eval_jaxpr/ppermute | solution.py:18
  37.2 5.4 %collective-permute-start = (f32[6,128]{1,0:T(8,128)S(1)}, f32[6,128]{1,0:T(8,128)S(1)}, u32[]{:S(2)}, u32[]{:S(2)}) collective-permute-start(f32[6,128]{1,0:T(8,128)S(1)} %copy.92), channel_id=1, source_target_pairs={{0,8},{8,16},{16,24},{24,0},{1,9},{9,17},{17,25},{25,1},{2,10},{10... | collective-permute-start | bytes 9224 | tf_op jit(solution)/shard_map/while/body/eval_jaxpr/ppermute | solution.py:18
  37.9 5.5 %collective-permute-start.1 = (f32[6,128]{1,0:T(8,128)S(1)}, f32[6,128]{1,0:T(8,128)S(1)}, u32[]{:S(2)}, u32[]{:S(2)}) collective-permute-start(f32[6,128]{1,0:T(8,128)S(1)} %maximum_add_fusion.2), channel_id=1, source_target_pairs={{0,8},{8,16},{16,24},{24,0},{1,9},{9,17},{17,25},{25,1},{2,10},{10... | collective-permute-start | bytes 9224 | tf_op jit(solution)/shard_map/while/body/eval_jaxpr/ppermute | solution.py:18
  43.4 5.4 %collective-permute-start = (f32[6,128]{1,0:T(8,128)S(1)}, f32[6,128]{1,0:T(8,128)S(1)}, u32[]{:S(2)}, u32[]{:S(2)}) collective-permute-start(f32[6,128]{1,0:T(8,128)S(1)} %copy.92), channel_id=1, source_target_pairs={{0,8},{8,16},{16,24},{24,0},{1,9},{9,17},{17,25},{25,1},{2,10},{10... | collective-permute-start | bytes 9224 | tf_op jit(solution)/shard_map/while/body/eval_jaxpr/ppermute | solution.py:18
  44.1 5.5 %collective-permute-start.1 = (f32[6,128]{1,0:T(8,128)S(1)}, f32[6,128]{1,0:T(8,128)S(1)}, u32[]{:S(2)}, u32[]{:S(2)}) collective-permute-start(f32[6,128]{1,0:T(8,128)S(1)} %maximum_add_fusion.2), channel_id=1, source_target_pairs={{0,8},{8,16},{16,24},{24,0},{1,9},{9,17},{17,25},{25,1},{2,10},{10... | collective-permute-start | bytes 9224 | tf_op jit(solution)/shard_map/while/body/eval_jaxpr/ppermute | solution.py:18
  49.6 5.4 %collective-permute-start = (f32[6,128]{1,0:T(8,128)S(1)}, f32[6,128]{1,0:T(8,128)S(1)}, u32[]{:S(2)}, u32[]{:S(2)}) collective-permute-start(f32[6,128]{1,0:T(8,128)S(1)} %copy.92), channel_id=1, source_target_pairs={{0,8},{8,16},{16,24},{24,0},{1,9},{9,17},{17,25},{25,1},{2,10},{10... | collective-permute-start | bytes 9224 | tf_op jit(solution)/shard_map/while/body/eval_jaxpr/ppermute | solution.py:18
  50.3 5.5 %collective-permute-start.1 = (f32[6,128]{1,0:T(8,128)S(1)}, f32[6,128]{1,0:T(8,128)S(1)}, u32[]{:S(2)}, u32[]{:S(2)}) collective-permute-start(f32[6,128]{1,0:T(8,128)S(1)} %maximum_add_fusion.2), channel_id=1, source_target_pairs={{0,8},{8,16},{16,24},{24,0},{1,9},{9,17},{17,25},{25,1},{2,10},{10... | collective-permute-start | bytes 9224 | tf_op jit(solution)/shard_map/while/body/eval_jaxpr/ppermute | solution.py:18
Sparse Core Ops, SparseCore 0:
  56.7 32.3 reduce-scatter.3
